TPU v7x, 32 devices: a whole 2x2x4 slice. The times are simulated.
32 devices in a mesh: wide: 8 (over z, core), narrow: 4 (over y, x).
Axes of the slice: x: 2, y: 2, z: 4, core: 2. Of those that a mesh axis runs over, the one named last changes fastest.
Arguments:
- tokens: bfloat16 [4096, 2048], P('wide'), may hold values from -6 to 6
- attn_gain: bfloat16 [2048], replicated, may hold values from 0.099609375 to 1.8984375
- w_query: bfloat16 [2048, 2048], P(None, 'narrow'), may hold values from -0.125 to 0.125
- w_key: bfloat16 [2048, 512], P(None, 'narrow'), may hold values from -0.125 to 0.125
- w_value: bfloat16 [2048, 512], P(None, 'narrow'), may hold values from -0.125 to 0.125
- w_out: bfloat16 [2048, 2048], P('narrow'), may hold values from -2 to 2
- ffn_gain: bfloat16 [2048], replicated, may hold values from 0.099609375 to 1.8984375
- w_gate: bfloat16 [2048, 8192], P(None, 'narrow'), may hold values from -0.125 to 0.125
- w_up: bfloat16 [2048, 8192], P(None, 'narrow'), may hold values from -0.125 to 0.125
- w_down: bfloat16 [8192, 2048], P('narrow'), may hold values from -0.0625 to 0.0625
- doc_lengths: int32 [12], replicated, may hold values from 1 to 2048, 4096 in all
- cotangent: bfloat16 [4096, 2048], P('wide'), may hold values from -6 to 6
Outputs:
- output: bfloat16 [4096, 2048], P('wide')
- input_grad: bfloat16 [4096, 2048], P('wide')
- grad_attn_gain: float32 [2048], P('wide')
- grad_query: float32 [2048, 2048], P('wide', 'narrow')
- grad_key: float32 [2048, 512], P('wide', 'narrow')
- grad_value: float32 [2048, 512], P('wide', 'narrow')
- grad_out: float32 [2048, 2048], P('narrow', 'wide')
- grad_ffn_gain: float32 [2048], P('wide')
- grad_gate: float32 [2048, 8192], P('wide', 'narrow')
- grad_up: float32 [2048, 8192], P('wide', 'narrow')
- grad_down: float32 [8192, 2048], P('narrow', 'wide')
Inputs may be any that keep to these rules, and one draw needn't show every extreme that they name: `doc_lengths`: the last entry is the padding at the row's end; the longest entry is exactly 2048.
All inputs are finite; a program needn't handle non-finite values.
Results may differ from a plain program's by a relative error of at most 0.02.
Values may be sent and summed in bfloat16 or wider, within the bound.
No kernel may reach another device: no remote copies, remote signals or barrier semaphores. Data moves between devices by JAX's collectives and lax.ppermute only.
A program may use at most 320 MiB of HBM per device.

v0:
```python
import math
import jax
import jax.numpy as jnp
import numpy as np
from jax import lax
from jax.sharding import PartitionSpec as P

HD = 64
QBLK = 512
DOCS = 12
NORM_EPS = 1e-05
MASKED_SCORE = -1e30


def inverse_frequencies(head_size):
    frequency = 1.0 / 500000.0 ** (np.arange(0, head_size, 2) / head_size)
    wavelength = 2 * math.pi / frequency
    smoothing = (8192.0 / wavelength - 1.0) / 3.0
    scaled_freq = np.where(wavelength > 8192.0, frequency / 32.0, frequency)
    middle_band = (wavelength <= 8192.0) & (wavelength >= 2048.0)
    scaled_freq = np.where(
        middle_band, (1 - smoothing) * frequency / 32.0 + smoothing * frequency, scaled_freq
    )
    return scaled_freq.astype(np.float32)


def doc_layout(doc_lengths, index):
    ends = jnp.cumsum(doc_lengths)
    passed = (index[:, None] >= ends[None, :]).astype(jnp.int32)
    segment = jnp.sum(passed, axis=1)
    offset = jnp.sum(passed * doc_lengths[None, :], axis=1)
    position = index - offset
    valid = index < ends[DOCS - 2]
    return (segment, position, valid)


def rotate(values, position, heads, direction):
    angle = position.astype(jnp.float32)[:, None] * jnp.asarray(inverse_frequencies(HD))[None, :]
    cosine = jnp.cos(angle)[:, None, :]
    sine = direction * jnp.sin(angle)[:, None, :]
    shaped = values.reshape(values.shape[0], heads, 2, HD // 2)
    first = shaped[:, :, 0]
    second = shaped[:, :, 1]
    return jnp.stack(
        [first * cosine - second * sine, second * cosine + first * sine], axis=2
    ).reshape(values.shape)


def contract_rows(left, right):
    return lax.dot_general(
        left, right, (((0,), (0,)), ((), ())), preferred_element_type=jnp.float32
    )


def contract_cols(left, right):
    return lax.dot_general(
        left, right, (((1,), (1,)), ((), ())), preferred_element_type=jnp.float32
    )


def head_scores(query_head, key_head, allowed):
    raw_scores = contract_cols(query_head, key_head)
    return jnp.where(allowed, raw_scores / math.sqrt(HD), MASKED_SCORE)


def norm_back(grad_normed, gain, values, inverse):
    scaled = grad_normed * gain
    return inverse * scaled - values * inverse**3 * jnp.mean(
        scaled * values, axis=-1, keepdims=True
    )


def body(
    tokens,
    attn_gain,
    w_query,
    w_key,
    w_value,
    w_out,
    ffn_gain,
    w_gate,
    w_up,
    w_down,
    doc_lengths,
    cotangent,
):
    rows = tokens.shape[0]
    total = rows * lax.axis_size("wide")
    heads = w_query.shape[1] // HD
    kv_heads = w_key.shape[1] // HD
    group = heads // kv_heads
    blocks = rows // QBLK
    local_index = lax.axis_index("wide") * rows + jnp.arange(rows, dtype=jnp.int32)
    segment, position, valid = doc_layout(doc_lengths, local_index)
    key_index = jnp.arange(total, dtype=jnp.int32)
    key_layout = doc_layout(doc_lengths, key_index)
    key_segment = key_layout[0]
    inputs = tokens.astype(jnp.float32)
    gain_one = attn_gain.astype(jnp.float32)
    gain_two = ffn_gain.astype(jnp.float32)
    inv_one = lax.rsqrt(jnp.mean(inputs * inputs, axis=-1, keepdims=True) + NORM_EPS)
    normed = (inputs * inv_one * gain_one).astype(jnp.bfloat16)
    query = jnp.dot(normed, w_query, preferred_element_type=jnp.float32)
    keys = jnp.dot(normed, w_key, preferred_element_type=jnp.float32)
    values = jnp.dot(normed, w_value, preferred_element_type=jnp.float32).astype(jnp.bfloat16)
    query_r = rotate(query, position, heads, 1.0).astype(jnp.bfloat16)
    keys_r = rotate(keys, position, kv_heads, 1.0).astype(jnp.bfloat16)
    packed = jnp.concatenate([keys_r, values], axis=1)
    gathered = lax.all_gather(packed, "wide", axis=0, tiled=True)
    width = kv_heads * HD
    all_keys = gathered[:, :width]
    all_values = gathered[:, width:]

    def block_mask(segment_block, index_block):
        return (segment_block[:, None] == key_segment[None, :]) & (
            index_block[:, None] >= key_index[None, :]
        )

    def attend(block_in):
        query_block, segment_block, index_block = block_in
        allowed = block_mask(segment_block, index_block)
        outputs = []
        totals = []
        for head in range(heads):
            column = head // group * HD
            scores = head_scores(
                query_block[:, head * HD : (head + 1) * HD],
                all_keys[:, column : column + HD],
                allowed,
            )
            row_max = jnp.max(scores, axis=1, keepdims=True)
            exponent = jnp.exp(scores - row_max)
            row_sum = jnp.sum(exponent, axis=1, keepdims=True)
            probs = (exponent / row_sum).astype(jnp.bfloat16)
            outputs.append(
                jnp.dot(
                    probs, all_values[:, column : column + HD], preferred_element_type=jnp.float32
                )
            )
            totals.append(row_max[:, 0] + jnp.log(row_sum[:, 0]))
        return (jnp.concatenate(outputs, axis=1), jnp.stack(totals, axis=1))

    query_blocks = query_r.reshape(blocks, QBLK, heads * HD)
    segment_blocks = segment.reshape(blocks, QBLK)
    index_blocks = local_index.reshape(blocks, QBLK)
    attended, log_sums = lax.map(attend, (query_blocks, segment_blocks, index_blocks))
    valid_rows = valid[:, None]
    mixed = jnp.where(valid_rows, attended.reshape(rows, heads * HD), 0.0).astype(jnp.bfloat16)
    attn_part = jnp.dot(mixed, w_out, preferred_element_type=jnp.float32)
    hidden_one = inputs + lax.psum(attn_part, "narrow")
    inv_two = lax.rsqrt(jnp.mean(hidden_one * hidden_one, axis=-1, keepdims=True) + NORM_EPS)
    normed_two = (hidden_one * inv_two * gain_two).astype(jnp.bfloat16)
    gate = jnp.dot(normed_two, w_gate, preferred_element_type=jnp.float32)
    up_proj = jnp.dot(normed_two, w_up, preferred_element_type=jnp.float32)
    sigmoid_gate = jax.nn.sigmoid(gate)
    silu_gate = gate * sigmoid_gate
    activ = (silu_gate * up_proj).astype(jnp.bfloat16)
    ffn_part = jnp.dot(activ, w_down, preferred_element_type=jnp.float32)
    grad_down = contract_rows(activ, cotangent)
    d_activ = contract_cols(cotangent, w_down)
    d_gate = (d_activ * up_proj * sigmoid_gate * (1.0 + gate * (1.0 - sigmoid_gate))).astype(
        jnp.bfloat16
    )
    d_up = (d_activ * silu_gate).astype(jnp.bfloat16)
    grad_gate = contract_rows(normed_two, d_gate)
    grad_up = contract_rows(normed_two, d_up)
    norm_two_part = contract_cols(d_gate, w_gate) + contract_cols(d_up, w_up)
    output = (
        hidden_one + lax.psum(ffn_part.astype(jnp.bfloat16), "narrow").astype(jnp.float32)
    ).astype(jnp.bfloat16)
    d_norm_two = lax.psum(norm_two_part.astype(jnp.bfloat16), "narrow").astype(jnp.float32)
    grad_ffn_gain = jnp.sum(d_norm_two * hidden_one * inv_two, axis=0)
    d_hidden = cotangent.astype(jnp.float32) + norm_back(d_norm_two, gain_two, hidden_one, inv_two)
    d_hidden_b = d_hidden.astype(jnp.bfloat16)
    grad_out = contract_rows(mixed, d_hidden_b)
    d_mixed = jnp.where(
        valid_rows,
        contract_cols(d_hidden_b, w_out).astype(jnp.bfloat16),
        jnp.zeros((), jnp.bfloat16),
    )

    def attend_back(carry, block_in):
        query_block, grad_block, lse_block, segment_block, index_block = block_in
        allowed = block_mask(segment_block, index_block)
        query_grads = []
        key_terms = [None] * kv_heads
        value_terms = [None] * kv_heads
        for head in range(heads):
            kv_index = head // group
            column = kv_index * HD
            query_head = query_block[:, head * HD : (head + 1) * HD]
            grad_head = grad_block[:, head * HD : (head + 1) * HD]
            key_head = all_keys[:, column : column + HD]
            value_head = all_values[:, column : column + HD]
            scores = head_scores(query_head, key_head, allowed)
            probs = jnp.where(allowed, jnp.exp(scores - lse_block[:, head : head + 1]), 0.0)
            prob_grad = contract_cols(grad_head, value_head)
            delta = jnp.sum(probs * prob_grad, axis=1, keepdims=True)
            d_scores = (probs * (prob_grad - delta)).astype(jnp.bfloat16)
            query_grads.append(
                jnp.dot(d_scores, key_head, preferred_element_type=jnp.float32) / math.sqrt(HD)
            )
            key_term = contract_rows(d_scores, query_head) / math.sqrt(HD)
            value_term = contract_rows(probs.astype(jnp.bfloat16), grad_head)
            if key_terms[kv_index] is None:
                key_terms[kv_index] = key_term
                value_terms[kv_index] = value_term
            else:
                key_terms[kv_index] = key_terms[kv_index] + key_term
                value_terms[kv_index] = value_terms[kv_index] + value_term
        update = jnp.concatenate(key_terms + value_terms, axis=1)
        return (carry + update, jnp.concatenate(query_grads, axis=1))

    start_terms = jnp.zeros((total, 2 * width), jnp.float32)
    grad_blocks = d_mixed.reshape(blocks, QBLK, heads * HD)
    kv_terms, query_grad_blocks = lax.scan(
        attend_back,
        start_terms,
        (query_blocks, grad_blocks, log_sums, segment_blocks, index_blocks),
    )
    d_kv = lax.psum_scatter(
        kv_terms.astype(jnp.bfloat16), "wide", scatter_dimension=0, tiled=True
    ).astype(jnp.float32)
    d_query = rotate(query_grad_blocks.reshape(rows, heads * HD), position, heads, -1.0).astype(
        jnp.bfloat16
    )
    d_keys = rotate(d_kv[:, :width], position, kv_heads, -1.0).astype(jnp.bfloat16)
    d_values = d_kv[:, width:].astype(jnp.bfloat16)
    grad_query = contract_rows(normed, d_query)
    grad_key = contract_rows(normed, d_keys)
    grad_value = contract_rows(normed, d_values)
    norm_one_part = (
        contract_cols(d_query, w_query)
        + contract_cols(d_keys, w_key)
        + contract_cols(d_values, w_value)
    )
    d_norm_one = lax.psum(norm_one_part.astype(jnp.bfloat16), "narrow").astype(jnp.float32)
    grad_attn_gain = jnp.sum(d_norm_one * inputs * inv_one, axis=0)
    input_grad = (d_hidden + norm_back(d_norm_one, gain_one, inputs, inv_one)).astype(jnp.bfloat16)
    summed = (
        lax.psum_scatter(
            grad_attn_gain.astype(jnp.bfloat16), "wide", scatter_dimension=0, tiled=True
        ).astype(jnp.float32),
        lax.psum_scatter(
            grad_query.astype(jnp.bfloat16), "wide", scatter_dimension=0, tiled=True
        ).astype(jnp.float32),
        lax.psum_scatter(
            grad_key.astype(jnp.bfloat16), "wide", scatter_dimension=0, tiled=True
        ).astype(jnp.float32),
        lax.psum_scatter(
            grad_value.astype(jnp.bfloat16), "wide", scatter_dimension=0, tiled=True
        ).astype(jnp.float32),
        lax.psum_scatter(
            grad_out.astype(jnp.bfloat16), "wide", scatter_dimension=1, tiled=True
        ).astype(jnp.float32),
        lax.psum_scatter(
            grad_ffn_gain.astype(jnp.bfloat16), "wide", scatter_dimension=0, tiled=True
        ).astype(jnp.float32),
        lax.psum_scatter(
            grad_gate.astype(jnp.bfloat16), "wide", scatter_dimension=0, tiled=True
        ).astype(jnp.float32),
        lax.psum_scatter(
            grad_up.astype(jnp.bfloat16), "wide", scatter_dimension=0, tiled=True
        ).astype(jnp.float32),
        lax.psum_scatter(
            grad_down.astype(jnp.bfloat16), "wide", scatter_dimension=1, tiled=True
        ).astype(jnp.float32),
    )
    gain_attn = summed[0]
    gain_ffn = summed[5]
    return (
        output,
        input_grad,
        gain_attn,
        summed[1],
        summed[2],
        summed[3],
        summed[4],
        gain_ffn,
        summed[6],
        summed[7],
        summed[8],
    )


def solution(mesh):
    in_specs = (
        P("wide", None),
        P(),
        P(None, "narrow"),
        P(None, "narrow"),
        P(None, "narrow"),
        P("narrow", None),
        P(),
        P(None, "narrow"),
        P(None, "narrow"),
        P("narrow", None),
        P(),
        P("wide", None),
    )
    out_specs = (
        P("wide", None),
        P("wide", None),
        P("wide"),
        P("wide", "narrow"),
        P("wide", "narrow"),
        P("wide", "narrow"),
        P("narrow", "wide"),
        P("wide"),
        P("wide", "narrow"),
        P("wide", "narrow"),
        P("narrow", "wide"),
    )
    return jax.shard_map(body, mesh=mesh, in_specs=in_specs, out_specs=out_specs, check_vma=False)
```

profile of v0, /device:TPU:0, one launch (start us, length us, event | category | flops | bytes accessed | tf_op | source)
XLA Modules:
  0.0 1095.4 jit_solution(12022537940424208202)
XLA Ops:
  12.5 2.6 convolution_convert_fusion.9
  19.5 3.6 fusion.159
  24.1 25.7 %all-gather.2.cloned.1.call-done = bf16[4096,256]{0,1:T(8,128)(2,1)} async-done(((bf16[512,256]{0,1:T(8,128)(2,1)}), bf16[4096,256]{0,1:T(8,128)(2,1)}) %all-gather.2.cloned.1.call-update) | async-done | bytes 2097168 | tf_op jit(solution)/shard_map/all_gather | solution.py:109
  49.8 3.6 fusion.176
  53.4 3.2 copy-done.7
  57.9 3.6 fusion.175
  62.9 4.1 fusion.174
  70.2 3.6 fusion.173
  77.1 3.6 fusion.172
  80.7 3.3 copy-done.10
  85.3 3.6 fusion.171
  90.2 4.5 fusion.170
  96.0 7.2 fusion.169
  103.1 4.8 fusion.1
  107.9 5.0 fusion.60
  116.7 5.4 fusion.57
  131.1 3.3 fusion.71
  134.7 103.2 %all-reduce.8.cloned.1.call-done = f32[512,2048]{1,0:T(8,128)} async-done(((f32[512,2048]{1,0:T(8,128)}), f32[512,2048]{1,0:T(8,128)}) %all-reduce.8.cloned.1.call-update) | async-done | bytes 4194320 | tf_op jit(solution)/shard_map/psum | solution.py:150
  237.9 3.5 multiply_reduce_fusion.8
  241.9 9.3 fusion.178
  251.2 6.3 fusion.177
  257.5 12.0 %multiply_convert_fusion.8 = (bf16[512,2048]{1,0:T(8,128)(2,1)}, bf16[512,2048]{1,0:T(8,128)(2,1)}, bf16[512,2048]{1,0:T(8,128)(2,1)}) fusion(f32[512,2048]{1,0:T(8,128)} %fusion.177, f32[512,2048]{1,0:T(8,128)S(1)} %fusion.178, bf16[512,2048]{1,0:T(8,128)(2,1)S(1)} %copy-done.36, bf16[2048,2048]{1,0:T(8,128)(2,1)} %param.25), kind=kOutput, calls=%fused_computation.118 | convolution fusion | flops 4310695936 | bytes 25165824 | tf_op jit(solution)/shard_map/dot_general | solution.py:56
  269.5 7.8 fusion.179
  277.3 9.4 add_convert_fusion.1
  287.2 69.3 %all-reduce.10.cloned.1.call-done = bf16[512,2048]{1,0:T(8,128)(2,1)} async-done(((bf16[512,2048]{1,0:T(8,128)(2,1)}), bf16[512,2048]{1,0:T(8,128)(2,1)}) %all-reduce.10.cloned.1.call-update) | async-done | bytes 2097168 | tf_op jit(solution)/shard_map/psum | solution.py:171
  356.5 4.9 fusion.25
  361.4 3.6 fusion.22
  376.2 2.6 convolution_add_fusion.4
  378.9 3.3 fusion.16
  387.2 3.3 fusion.17
  390.5 4.6 fusion.78
  395.0 4.6 fusion.80
  399.6 4.9 fusion.94
  405.8 4.6 fusion.98
  410.4 4.5 fusion.100
  415.0 26.5 %multiply_reduce_fusion = (f32[512]{0:T(512)S(1)}, f32[512]{0:T(512)S(1)}, f32[512]{0:T(512)S(1)}, f32[512]{0:T(512)S(1)}, f32[512]{0:T(512)S(1)}, /*index=5*/f32[512,4096]{1,0:T(8,128)}) fusion(f32[512,4096]{1,0:T(8,128)} %copy-done.7, f32[512]{0:T(512)S(1)} %log_add_fusion, s32[512]{0:T(512)S(1)} %iota_add_fusion, s32[4096]{0:T(1024)S(1)} %convert_reduce_fusion, ...), kind=kOutput, calls=%fused_computation.7 | convolution fusion | flops 316667392 | bytes 84516864 | tf_op jit(solution)/shard_map/while/body/eval_jaxpr/dot_general | solution.py:56
  441.5 25.5 %multiply_reduce_fusion.1 = (f32[512]{0:T(512)S(1)}, f32[512]{0:T(512)S(1)}, f32[512]{0:T(512)S(1)}, bf16[512,4096]{1,0:T(8,128)(2,1)}, f32[512,4096]{1,0:T(8,128)}) fusion(f32[512,4096]{1,0:T(8,128)} %copy-done.4, f32[512]{0:T(512)S(1)} %get-tuple-element.145, s32[512]{0:T(512)S(1)} %iota_add_fusion, s32[4096]{0:T(1024)S(1)} %convert_reduce_fusion, ...), kind=kOutput, calls=%fused_computation.10 | convolution fusion | flops 310376960 | bytes 71929856 | tf_op jit(solution)/shard_map/while/body/eval_jaxpr/dot_general | solution.py:56
  467.0 21.2 %multiply_convert_fusion.2 = (bf16[512,4096]{1,0:T(8,128)(2,1)}, bf16[512,4096]{1,0:T(8,128)(2,1)}, bf16[512,4096]{1,0:T(8,128)(2,1)S(1)}) fusion(f32[512,4096]{1,0:T(8,128)} %fusion.78, f32[512]{0:T(512)S(1)} %get-tuple-element.88, f32[512,4096]{1,0:T(8,128)} %copy-done.8, f32[512]{0:T(512)S(1)} %get-tuple-element.146, s32[512]{0:T(512)S(1)} %iota_add_fusion, ...), kind=kLoop, calls=%fused_computation.12 | loop fusion | flops 37748736 | bytes 62947328 | tf_op jit(solution)/shard_map/while/body/eval_jaxpr/convert_element_type | solution.py:199
  492.1 27.0 %multiply_convert_fusion.1 = (bf16[512,4096]{1,0:T(8,128)(2,1)}, bf16[512,4096]{1,0:T(8,128)(2,1)}, bf16[512,4096]{1,0:T(8,128)(2,1)}, bf16[512,4096]{1,0:T(8,128)(2,1)}) fusion(f32[512,4096]{1,0:T(8,128)} %get-tuple-element.140, f32[512]{0:T(512)S(1)} %get-tuple-element.74, f32[512,4096]{1,0:T(8,128)} %copy-done.4, f32[512]{0:T(512)S(1)} %get-tuple-element.145, ...), kind=kLoop, calls=%fused_computation.9 | loop fusion | flops 48234496 | bytes 83922944 | tf_op jit(solution)/shard_map/while/body/eval_jaxpr/convert_element_type | solution.py:199
  519.2 3.2 fusion.145
  533.6 4.7 convolution_convert_fusion.3
  538.4 3.9 fusion.68
  542.4 3.7 fusion.67
  555.0 2.9 convolution_convert_fusion.4
  558.0 11.5 %reduce-scatter.9.cloned.1.call-done = bf16[512,256]{0,1:T(8,128)(2,1)} async-done(((bf16[4096,256]{0,1:T(8,128)(2,1)}), bf16[512,256]{0,1:T(8,128)(2,1)}) %reduce-scatter.9.cloned.1.call-update) | async-done | bytes 262160 | tf_op jit(solution)/shard_map/reduce_scatter | solution.py:221
  572.8 10.0 convolution_convert_fusion.5
  584.8 3.0 fusion.180
  591.0 10.1 convolution_convert_fusion.1
  601.3 10.1 convolution_convert_fusion.2
  611.4 10.3 convolution_convert_fusion
  625.4 17.5 %reduce-scatter.11.cloned.1.call-done = bf16[256,512]{1,0:T(8,128)(2,1)} async-done(((bf16[2048,512]{1,0:T(8,128)(2,1)}), bf16[256,512]{1,0:T(8,128)(2,1)}) %reduce-scatter.11.cloned.1.call-update) | async-done | bytes 262160 | tf_op jit(solution)/shard_map/reduce_scatter | solution.py:244
  644.7 30.1 %reduce-scatter.13.cloned.1.call-done = bf16[256,128]{1,0:T(8,128)(2,1)} async-done(((bf16[2048,128]{1,0:T(8,128)(2,1)}), bf16[256,128]{1,0:T(8,128)(2,1)}) %reduce-scatter.13.cloned.1.call-update) | async-done | bytes 65552 | tf_op jit(solution)/shard_map/reduce_scatter | solution.py:247
  676.2 30.1 %reduce-scatter.15.cloned.1.call-done = bf16[256,128]{1,0:T(8,128)(2,1)} async-done(((bf16[2048,128]{1,0:T(8,128)(2,1)}), bf16[256,128]{1,0:T(8,128)(2,1)}) %reduce-scatter.15.cloned.1.call-update) | async-done | bytes 65552 | tf_op jit(solution)/shard_map/reduce_scatter | solution.py:250
  707.8 105.0 %all-reduce.12.cloned.1.call-done = (bf16[512,2048]{1,0:T(8,128)(2,1)}, bf16[512,2048]{1,0:T(8,128)(2,1)}) async-done(((bf16[512,2048]{1,0:T(8,128)(2,1)}, bf16[512,2048]{1,0:T(8,128)(2,1)}), (bf16[512,2048]{1,0:T(8,128)(2,1)}, bf16[512,2048]{1,0:T(8,128)(2,1)})) %all-reduce.12.cloned.1.call-update) | async-done | bytes 4194320 | tf_op jit(solution)/shard_map/psum | solution.py:169
  812.8 3.2 fusion.32
  816.0 17.4 %all-reduce.2 = (bf16[2048]{0:T(1024)(128)(2,1)S(1)}, bf16[2048]{0:T(1024)(128)(2,1)S(1)}) all-reduce(bf16[2048]{0:T(1024)(128)(2,1)S(1)} %get-tuple-element.67, bf16[2048]{0:T(1024)(128)(2,1)S(1)} %copy-done.52), channel_id=3, replica_groups=mesh['wide'=8,'narrow'=4] {'wide'}, use_global_device_ids=true, to_apply=%region_38.39.clone | all-reduce | flops 4096 | bytes 16384
  834.7 5.1 add_convert_fusion.2
  840.9 2.6 fusion.20
  843.5 61.7 %reduce-scatter.21.cloned.1.call-done = bf16[256,2048]{1,0:T(8,128)(2,1)} async-done(((bf16[2048,2048]{1,0:T(8,128)(2,1)}), bf16[256,2048]{1,0:T(8,128)(2,1)}) %reduce-scatter.21.cloned.1.call-update) | async-done | bytes 1048592 | tf_op jit(solution)/shard_map/reduce_scatter | solution.py:262
  905.2 2.8 convert_element_type.315
  908.0 87.4 %reduce-scatter.19.cloned.1.call-done = bf16[256,2048]{1,0:T(8,128)(2,1)} async-done(((bf16[2048,2048]{1,0:T(8,128)(2,1)}), bf16[256,2048]{1,0:T(8,128)(2,1)}) %reduce-scatter.19.cloned.1.call-update) | async-done | bytes 1048592 | tf_op jit(solution)/shard_map/reduce_scatter | solution.py:259
  995.4 2.8 convert_element_type.313
  998.2 87.4 %reduce-scatter.23.cloned.1.call-done = bf16[2048,256]{1,0:T(8,128)(2,1)} async-done(((bf16[2048,2048]{1,0:T(8,128)(2,1)}), bf16[2048,256]{1,0:T(8,128)(2,1)}) %reduce-scatter.23.cloned.1.call-update) | async-done | bytes 1048592 | tf_op jit(solution)/shard_map/reduce_scatter | solution.py:265
  1085.7 2.7 convert_element_type.317
  (281 shorter events, 97.3 us)
Async XLA Ops:
  7.2 123.9 %copy-start = (bf16[512,2048]{1,0:T(8,128)(2,1)S(1)}, bf16[512,2048]{1,0:T(8,128)(2,1)}, u32[]{:S(2)}) copy-start(bf16[512,2048]{1,0:T(8,128)(2,1)} %param.21) | copy-start | bytes 6291460
  7.2 7.9 copy-start.40
  7.2 42.6 %all-gather.2.cloned.1.call-start = ((), (), s32[]{:S(2)}) async-start(), calls=%async_computation.8 | async-start | bytes 2359296 | tf_op jit(solution)/shard_map/all_gather | solution.py:109
  10.1 9.4 copy-start.50
  10.9 4.2 copy-start.26
  12.5 6.9 copy-start.48
  12.5 3.6 copy-start.57
  17.0 6.0 copy-start.37
  17.9 220.0 %all-reduce.8.cloned.1.call-start = ((), (), s32[]{:S(2)}) async-start(), calls=%async_computation.9 | async-start | bytes 8388608 | tf_op jit(solution)/shard_map/psum | solution.py:150
  19.3 345.7 %copy-start.53 = (pred[512]{0:T(512)(128)(4,1)}, pred[512]{0:T(512)(128)(4,1)S(1)}, u32[]{:S(2)}) copy-start(pred[512]{0:T(512)(128)(4,1)S(1)} %fusion.150) | copy-start | bytes 1540
  61.6 64.6 %copy-start.4 = (f32[512,4096]{1,0:T(8,128)}, f32[512,4096]{1,0:T(8,128)S(1)}, u32[]{:S(2)}) copy-start(f32[512,4096]{1,0:T(8,128)S(1)} %get-tuple-element.136) | copy-start | bytes 25165828
  66.9 3.3 copy-start.8
  88.9 25.9 %copy-start.5 = (f32[512,4096]{1,0:T(8,128)}, f32[512,4096]{1,0:T(8,128)S(1)}, u32[]{:S(2)}) copy-start(f32[512,4096]{1,0:T(8,128)S(1)} %get-tuple-element.128) | copy-start | bytes 25165828
  94.7 18.3 %copy-start.6 = (f32[512,4096]{1,0:T(8,128)}, f32[512,4096]{1,0:T(8,128)S(1)}, u32[]{:S(2)}) copy-start(f32[512,4096]{1,0:T(8,128)S(1)} %get-tuple-element.126) | copy-start | bytes 25165828
  103.1 4.8 copy-start.24
  114.8 7.2 slice-start.16
  116.6 5.4 slice-start.17
  116.7 7.2 slice-start.10
  124.4 3.7 slice-start.6
  131.1 3.6 copy-start.56
  134.4 222.1 %all-reduce.10.cloned.1.call-start = ((), (), s32[]{:S(2)}) async-start(), calls=%async_computation.10 | async-start | bytes 4194304 | tf_op jit(solution)/shard_map/psum | solution.py:171
  241.4 9.8 copy-start.2
  241.4 9.8 slice-start.22
  241.8 9.4 copy-start.35
  241.8 9.4 slice-start.23
  251.2 6.3 copy-start.36
  269.5 7.8 copy-start.59
  286.7 282.8 %reduce-scatter.9.cloned.1.call-start = ((), (), s32[]{:S(2)}) async-start(), calls=%async_computation.11 | async-start | bytes 2359296 | tf_op jit(solution)/shard_map/reduce_scatter | solution.py:221
  356.5 4.9 copy-start.3
  356.5 10.7 slice-start.14
  361.4 5.8 slice-start.15
  365.1 4.6 slice-start.18
  367.2 5.4 slice-start.4
  370.2 4.9 slice-start.2
  370.2 8.7 slice-start.20
  372.7 3.6 slice-start.3
  372.7 6.2 slice-start.21
  376.2 6.0 slice-start.12
  376.2 8.4 slice-start
  378.9 3.3 slice-start.13
  378.9 5.8 slice-start.1
  382.2 4.9 slice-start.8
  387.2 3.3 copy-start.25
  467.0 23.3 %copy-start.34 = (bf16[512,8,2,32]{0,3,2,1:T(8,128)(2,1)S(1)}, bf16[512,8,2,32]{0,3,2,1:T(8,128)(2,1)}, u32[]{:S(2)}) copy-start(bf16[512,8,2,32]{0,3,2,1:T(8,128)(2,1)} %pad_maximum_fusion.1) | copy-start | bytes 1572868
  519.1 3.5 copy-start.13
  519.1 3.7 copy-start.33
  533.5 90.1 %reduce-scatter.17.cloned.1.call-start = ((), (), s32[]{:S(2)}) async-start(), calls=%async_computation.15 | async-start | bytes 2359296 | tf_op jit(solution)/shard_map/reduce_scatter | solution.py:253
  538.4 104.5 %reduce-scatter.11.cloned.1.call-start = ((), (), s32[]{:S(2)}) async-start(), calls=%async_computation.12 | async-start | bytes 2359296 | tf_op jit(solution)/shard_map/reduce_scatter | solution.py:244
  538.4 7.7 copy-start.22
  542.3 5.2 copy-start.18
  555.0 15.5 %copy-start.28 = (bf16[512,2048]{1,0:T(8,128)(2,1)S(1)}, bf16[512,2048]{1,0:T(8,128)(2,1)}, u32[]{:S(2)}) copy-start(bf16[512,2048]{1,0:T(8,128)(2,1)} %param.16) | copy-start | bytes 6291460
  557.9 116.8 %reduce-scatter.13.cloned.1.call-start = ((), (), s32[]{:S(2)}) async-start(), calls=%async_computation.13 | async-start | bytes 589824 | tf_op jit(solution)/shard_map/reduce_scatter | solution.py:247
  572.4 133.9 %reduce-scatter.15.cloned.1.call-start = ((), (), s32[]{:S(2)}) async-start(), calls=%async_computation.14 | async-start | bytes 589824 | tf_op jit(solution)/shard_map/reduce_scatter | solution.py:250
  572.8 10.1 copy-start.47
  584.7 228.1 %all-reduce.12.cloned.1.call-start = ((), (), s32[]{:S(2)}) async-start(), calls=%async_computation.19 | async-start | bytes 8388608 | tf_op jit(solution)/shard_map/psum | solution.py:169
  590.9 314.3 %reduce-scatter.21.cloned.1.call-start = ((), (), s32[]{:S(2)}) async-start(), calls=%async_computation.17 | async-start | bytes 9437184 | tf_op jit(solution)/shard_map/reduce_scatter | solution.py:262
  601.1 394.3 %reduce-scatter.19.cloned.1.call-start = ((), (), s32[]{:S(2)}) async-start(), calls=%async_computation.16 | async-start | bytes 9437184 | tf_op jit(solution)/shard_map/reduce_scatter | solution.py:259
  611.4 474.3 %reduce-scatter.23.cloned.1.call-start = ((), (), s32[]{:S(2)}) async-start(), calls=%async_computation.18 | async-start | bytes 9437184 | tf_op jit(solution)/shard_map/reduce_scatter | solution.py:265
  621.7 194.2 %copy-start.52 = (bf16[2048]{0:T(1024)(128)(2,1)S(1)}, bf16[2048]{0:T(1024)(128)(2,1)}, u32[]{:S(2)}) copy-start(bf16[2048]{0:T(1024)(128)(2,1)} %get-tuple-element.65) | copy-start | bytes 12292
  642.9 196.9 %copy-start.55 = (f32[512]{0:T(512)S(1)}, f32[512]{0:T(512)}, u32[]{:S(2)}) copy-start(f32[512]{0:T(512)} %get-tuple-element.119) | copy-start | bytes 6148
  834.7 5.1 copy-start.29
  834.7 5.1 copy-start.31
  834.7 6.2 copy-start.32
  840.9 247.5 %copy-start.1 = (bf16[512,2048]{1,0:T(8,128)(2,1)S(1)}, bf16[512,2048]{1,0:T(8,128)(2,1)}, u32[]{:S(2)}) copy-start(bf16[512,2048]{1,0:T(8,128)(2,1)} %param.21) | copy-start | bytes 6291460
  (32 other events, 72.7 us)
Sparse Core Ops, SparseCore 0:
  18.0 31.7 all-gather.1
  134.5 103.3 all-reduce.7
  286.8 69.6 all-reduce.9
  533.6 35.8 reduce-scatter.8
  571.6 34.4 reduce-scatter.16
  608.3 34.5 reduce-scatter.10
  645.1 29.5 reduce-scatter.12
  677.1 29.1 reduce-scatter.14
  710.4 102.3 all-reduce.11
  815.0 90.1 reduce-scatter.20
  907.6 87.7 reduce-scatter.18
  997.7 87.9 reduce-scatter.22
where the time goes:
time: 1100 us
  waiting for transfers between devices  629 us (57%)
  matrix products  293 us (27%)
  other arithmetic  112 us (10%)
  local copies, waits for them, and re-layouts  25.3 us (2%)
  blocking collectives  17.4 us (2%)
  between operations  16.3 us (1%)
    dot_general x23, matrix products, contract_cols(): lax.dot_general(left, right, (((1,), (1,)), ((), ())), preferred_element_...  147 us
    psum x1, waiting for transfers between devices, body(): lax.psum(ffn_part.astype(jnp.bfloat16), 'narrow').astype(jnp.float32)  105 us
    psum x1, waiting for transfers between devices, body(): hidden_one = inputs + lax.psum(attn_part, 'narrow')  103 us
    reduce_scatter x1, waiting for transfers between devices, body(): lax.psum_scatter(grad_down.astype(jnp.bfloat16), 'wide', scatter_dimensio...  87.4 us
    reduce_scatter x1, waiting for transfers between devices, body(): lax.psum_scatter(grad_gate.astype(jnp.bfloat16), 'wide', scatter_dimensio...  87.4 us
    dot_general x23, matrix products, contract_rows(): lax.dot_general(left, right, (((0,), (0,)), ((), ())), preferred_element_...  73.2 us
    psum x1, waiting for transfers between devices, body(): lax.psum(norm_two_part.astype(jnp.bfloat16), 'narrow').astype(jnp.float32)  69.3 us
    reduce_scatter x1, waiting for transfers between devices, body(): lax.psum_scatter(grad_up.astype(jnp.bfloat16), 'wide', scatter_dimension=...  61.7 us
  transfers between devices with their start and end apart: 12, of which 11 were waited for; matrix products, arithmetic and copies ran while one was open for 10% of the time, Pallas kernels for 0%

commit v1 on v0

--- a/solution.py
+++ b/solution.py
@@ -4,6 +4,7 @@
 import numpy as np
 from jax import lax
 from jax.sharding import PartitionSpec as P
+from jax.lax import all_gather
 
 HD = 64
 QBLK = 512
@@ -147,7 +148,10 @@
     valid_rows = valid[:, None]
     mixed = jnp.where(valid_rows, attended.reshape(rows, heads * HD), 0.0).astype(jnp.bfloat16)
     attn_part = jnp.dot(mixed, w_out, preferred_element_type=jnp.float32)
-    hidden_one = inputs + lax.psum(attn_part, "narrow")
+    _switch_spots = lambda local_block, comm_axis: jnp.sum(
+        all_gather(local_block, axis_name=comm_axis), axis=0
+    )
+    hidden_one = inputs + _switch_spots(attn_part, comm_axis="narrow")
     inv_two = lax.rsqrt(jnp.mean(hidden_one * hidden_one, axis=-1, keepdims=True) + NORM_EPS)
     normed_two = (hidden_one * inv_two * gain_two).astype(jnp.bfloat16)
     gate = jnp.dot(normed_two, w_gate, preferred_element_type=jnp.float32)

time: 1100 us -> 1160 us (1.055)
  waiting for transfers between devices: 629 us -> 683 us
    all_gather x0 -> x1, waiting for transfers between devices: none -> 157 us  [body(): all_gather(local_block, axis_name=comm_axis)]
    psum x1 -> x0, waiting for transfers between devices: 103 us -> none  [body(): hidden_one = inputs + lax.psum(attn_part, 'narrow')]
  transfers between devices with their start and end apart: 12 -> 12, of which waited for: 11 -> 11; matrix products, arithmetic and copies ran while one was open for 10% -> 9% of each run, Pallas kernels for 0% -> 0%
where the time goes in v1:
time: 1160 us
  waiting for transfers between devices  683 us (59%)
  matrix products  294 us (25%)
  other arithmetic  122 us (11%)
  local copies, waits for them, and re-layouts  25.4 us (2%)
  blocking collectives  17.4 us (1%)
  between operations  16.3 us (1%)
    all_gather x1, waiting for transfers between devices, body(): all_gather(local_block, axis_name=comm_axis)  157 us
    dot_general x23, matrix products, contract_cols(): lax.dot_general(left, right, (((1,), (1,)), ((), ())), preferred_element_...  147 us
    psum x1, waiting for transfers between devices, body(): lax.psum(ffn_part.astype(jnp.bfloat16), 'narrow').astype(jnp.float32)  105 us
    reduce_scatter x1, waiting for transfers between devices, body(): lax.psum_scatter(grad_gate.astype(jnp.bfloat16), 'wide', scatter_dimensio...  87.4 us
    reduce_scatter x1, waiting for transfers between devices, body(): lax.psum_scatter(grad_down.astype(jnp.bfloat16), 'wide', scatter_dimensio...  87.3 us
    dot_general x23, matrix products, contract_rows(): lax.dot_general(left, right, (((0,), (0,)), ((), ())), preferred_element_...  73.2 us
    psum x1, waiting for transfers between devices, body(): lax.psum(norm_two_part.astype(jnp.bfloat16), 'narrow').astype(jnp.float32)  69.3 us
    reduce_scatter x1, waiting for transfers between devices, body(): lax.psum_scatter(grad_up.astype(jnp.bfloat16), 'wide', scatter_dimension=...  61.6 us
  transfers between devices with their start and end apart: 12, of which 11 were waited for; matrix products, arithmetic and copies ran while one was open for 9% of the time, Pallas kernels for 0%

profile of v1, /device:TPU:0, one launch (start us, length us, event | category | flops | bytes accessed | tf_op | source)
XLA Modules:
  0.0 1159.7 jit_solution(1520132969177941962)
XLA Ops:
  19.5 3.6 fusion.159
  24.1 25.7 %all-gather.4.cloned.1.call-done = bf16[4096,256]{0,1:T(8,128)(2,1)} async-done(((bf16[512,256]{0,1:T(8,128)(2,1)}), bf16[4096,256]{0,1:T(8,128)(2,1)}) %all-gather.4.cloned.1.call-update) | async-done | bytes 2097168 | tf_op jit(solution)/shard_map/all_gather | solution.py:110
  49.8 3.6 fusion.176
  53.4 3.3 copy-done.7
  58.0 3.6 fusion.175
  63.0 4.1 fusion.174
  70.3 3.6 fusion.173
  77.2 3.6 fusion.172
  80.8 3.3 copy-done.10
  85.3 3.6 fusion.171
  90.3 4.5 fusion.170
  96.1 7.1 fusion.169
  103.2 4.8 fusion.1
  108.0 5.0 fusion.60
  116.7 5.4 fusion.57
  131.2 3.3 fusion.71
  134.6 157.0 %all-gather.6.cloned.1.call-done = f32[2048,2048]{1,0:T(8,128)} async-done(((f32[512,2048]{1,0:T(8,128)}), f32[2048,2048]{1,0:T(8,128)}) %all-gather.6.cloned.1.call-update) | async-done | bytes 16777232 | tf_op jit(solution)/shard_map/all_gather | solution.py:152
  291.6 10.2 reduce_sum.262
  301.7 3.5 multiply_reduce_fusion.8
  305.7 9.6 fusion.178
  315.4 6.3 fusion.177
  321.6 12.0 %multiply_convert_fusion.8 = (bf16[512,2048]{1,0:T(8,128)(2,1)}, bf16[512,2048]{1,0:T(8,128)(2,1)}, bf16[512,2048]{1,0:T(8,128)(2,1)}) fusion(f32[512,2048]{1,0:T(8,128)} %fusion.177, f32[512,2048]{1,0:T(8,128)S(1)} %fusion.178, bf16[512,2048]{1,0:T(8,128)(2,1)S(1)} %copy-done.36, bf16[2048,2048]{1,0:T(8,128)(2,1)} %param.25), kind=kOutput, calls=%fused_computation.118 | convolution fusion | flops 4310695936 | bytes 25165824 | tf_op jit(solution)/shard_map/dot_general | solution.py:57
  333.6 7.8 fusion.179
  341.4 9.4 add_convert_fusion.1
  351.4 69.3 %all-reduce.7.cloned.1.call-done = bf16[512,2048]{1,0:T(8,128)(2,1)} async-done(((bf16[512,2048]{1,0:T(8,128)(2,1)}), bf16[512,2048]{1,0:T(8,128)(2,1)}) %all-reduce.7.cloned.1.call-update) | async-done | bytes 2097168 | tf_op jit(solution)/shard_map/psum | solution.py:175
  420.7 4.9 fusion.25
  425.6 3.6 fusion.22
  440.4 2.6 convolution_add_fusion.4
  443.1 3.3 fusion.16
  451.3 3.3 fusion.17
  454.6 4.6 fusion.78
  459.2 4.6 fusion.80
  463.8 4.9 fusion.94
  470.0 4.5 fusion.98
  474.5 4.6 fusion.100
  479.1 26.5 %multiply_reduce_fusion = (f32[512]{0:T(512)S(1)}, f32[512]{0:T(512)S(1)}, f32[512]{0:T(512)S(1)}, f32[512]{0:T(512)S(1)}, f32[512]{0:T(512)S(1)}, /*index=5*/f32[512,4096]{1,0:T(8,128)}) fusion(f32[512,4096]{1,0:T(8,128)} %copy-done.7, f32[512]{0:T(512)S(1)} %log_add_fusion, s32[512]{0:T(512)S(1)} %iota_add_fusion, s32[4096]{0:T(1024)S(1)} %convert_reduce_fusion, ...), kind=kOutput, calls=%fused_computation.7 | convolution fusion | flops 316667392 | bytes 84516864 | tf_op jit(solution)/shard_map/while/body/eval_jaxpr/dot_general | solution.py:57
  505.6 25.6 %multiply_reduce_fusion.1 = (f32[512]{0:T(512)S(1)}, f32[512]{0:T(512)S(1)}, f32[512]{0:T(512)S(1)}, bf16[512,4096]{1,0:T(8,128)(2,1)}, f32[512,4096]{1,0:T(8,128)}) fusion(f32[512,4096]{1,0:T(8,128)} %copy-done.4, f32[512]{0:T(512)S(1)} %get-tuple-element.145, s32[512]{0:T(512)S(1)} %iota_add_fusion, s32[4096]{0:T(1024)S(1)} %convert_reduce_fusion, ...), kind=kOutput, calls=%fused_computation.10 | convolution fusion | flops 310376960 | bytes 71929856 | tf_op jit(solution)/shard_map/while/body/eval_jaxpr/dot_general | solution.py:57
  531.2 21.3 %multiply_convert_fusion.2 = (bf16[512,4096]{1,0:T(8,128)(2,1)}, bf16[512,4096]{1,0:T(8,128)(2,1)}, bf16[512,4096]{1,0:T(8,128)(2,1)S(1)}) fusion(f32[512,4096]{1,0:T(8,128)} %fusion.78, f32[512]{0:T(512)S(1)} %get-tuple-element.88, f32[512,4096]{1,0:T(8,128)} %copy-done.8, f32[512]{0:T(512)S(1)} %get-tuple-element.146, s32[512]{0:T(512)S(1)} %iota_add_fusion, ...), kind=kLoop, calls=%fused_computation.12 | loop fusion | flops 37748736 | bytes 62947328 | tf_op jit(solution)/shard_map/while/body/eval_jaxpr/convert_element_type | solution.py:203
  556.3 27.1 %multiply_convert_fusion.1 = (bf16[512,4096]{1,0:T(8,128)(2,1)}, bf16[512,4096]{1,0:T(8,128)(2,1)}, bf16[512,4096]{1,0:T(8,128)(2,1)}, bf16[512,4096]{1,0:T(8,128)(2,1)}) fusion(f32[512,4096]{1,0:T(8,128)} %get-tuple-element.140, f32[512]{0:T(512)S(1)} %get-tuple-element.74, f32[512,4096]{1,0:T(8,128)} %copy-done.4, f32[512]{0:T(512)S(1)} %get-tuple-element.145, ...), kind=kLoop, calls=%fused_computation.9 | loop fusion | flops 48234496 | bytes 83922944 | tf_op jit(solution)/shard_map/while/body/eval_jaxpr/convert_element_type | solution.py:203
  583.4 3.2 fusion.145
  597.8 4.8 convolution_convert_fusion.3
  602.7 3.9 fusion.68
  606.7 3.7 fusion.67
  619.3 2.9 convolution_convert_fusion.4
  622.3 11.4 reduce-scatter.9.cloned.1.call-done
  637.0 10.0 convolution_convert_fusion.5
  649.0 3.0 fusion.180
  655.1 10.1 convolution_convert_fusion.1
  665.5 10.1 convolution_convert_fusion.2
  675.6 10.3 convolution_convert_fusion
  689.6 17.5 %reduce-scatter.11.cloned.1.call-done = bf16[256,512]{1,0:T(8,128)(2,1)} async-done(((bf16[2048,512]{1,0:T(8,128)(2,1)}), bf16[256,512]{1,0:T(8,128)(2,1)}) %reduce-scatter.11.cloned.1.call-update) | async-done | bytes 262160 | tf_op jit(solution)/shard_map/reduce_scatter | solution.py:248
  708.9 30.2 %reduce-scatter.13.cloned.1.call-done = bf16[256,128]{1,0:T(8,128)(2,1)} async-done(((bf16[2048,128]{1,0:T(8,128)(2,1)}), bf16[256,128]{1,0:T(8,128)(2,1)}) %reduce-scatter.13.cloned.1.call-update) | async-done | bytes 65552 | tf_op jit(solution)/shard_map/reduce_scatter | solution.py:251
  740.5 29.9 %reduce-scatter.15.cloned.1.call-done = bf16[256,128]{1,0:T(8,128)(2,1)} async-done(((bf16[2048,128]{1,0:T(8,128)(2,1)}), bf16[256,128]{1,0:T(8,128)(2,1)}) %reduce-scatter.15.cloned.1.call-update) | async-done | bytes 65552 | tf_op jit(solution)/shard_map/reduce_scatter | solution.py:254
  771.9 105.4 %all-reduce.9.cloned.1.call-done = (bf16[512,2048]{1,0:T(8,128)(2,1)}, bf16[512,2048]{1,0:T(8,128)(2,1)}) async-done(((bf16[512,2048]{1,0:T(8,128)(2,1)}, bf16[512,2048]{1,0:T(8,128)(2,1)}), (bf16[512,2048]{1,0:T(8,128)(2,1)}, bf16[512,2048]{1,0:T(8,128)(2,1)})) %all-reduce.9.cloned.1.call-update) | async-done | bytes 4194320 | tf_op jit(solution)/shard_map/psum | solution.py:173
  877.4 3.2 fusion.32
  880.6 17.4 %all-reduce.2 = (bf16[2048]{0:T(1024)(128)(2,1)S(1)}, bf16[2048]{0:T(1024)(128)(2,1)S(1)}) all-reduce(bf16[2048]{0:T(1024)(128)(2,1)S(1)} %get-tuple-element.67, bf16[2048]{0:T(1024)(128)(2,1)S(1)} %copy-done.52), channel_id=4, replica_groups=mesh['wide'=8,'narrow'=4] {'wide'}, use_global_device_ids=true, to_apply=%region_38.39.clone | all-reduce | flops 4096 | bytes 16384
  899.2 5.1 add_convert_fusion.2
  905.4 2.6 fusion.20
  908.0 61.6 %reduce-scatter.21.cloned.1.call-done = bf16[256,2048]{1,0:T(8,128)(2,1)} async-done(((bf16[2048,2048]{1,0:T(8,128)(2,1)}), bf16[256,2048]{1,0:T(8,128)(2,1)}) %reduce-scatter.21.cloned.1.call-update) | async-done | bytes 1048592 | tf_op jit(solution)/shard_map/reduce_scatter | solution.py:266
  969.6 2.8 convert_element_type.315
  972.4 87.4 %reduce-scatter.19.cloned.1.call-done = bf16[256,2048]{1,0:T(8,128)(2,1)} async-done(((bf16[2048,2048]{1,0:T(8,128)(2,1)}), bf16[256,2048]{1,0:T(8,128)(2,1)}) %reduce-scatter.19.cloned.1.call-update) | async-done | bytes 1048592 | tf_op jit(solution)/shard_map/reduce_scatter | solution.py:263
  1059.8 2.8 convert_element_type.313
  1062.6 87.3 %reduce-scatter.23.cloned.1.call-done = bf16[2048,256]{1,0:T(8,128)(2,1)} async-done(((bf16[2048,2048]{1,0:T(8,128)(2,1)}), bf16[2048,256]{1,0:T(8,128)(2,1)}) %reduce-scatter.23.cloned.1.call-update) | async-done | bytes 1048592 | tf_op jit(solution)/shard_map/reduce_scatter | solution.py:269
  1150.0 2.7 convert_element_type.317
  (282 shorter events, 99.7 us)
Async XLA Ops:
  7.2 124.0 %copy-start = (bf16[512,2048]{1,0:T(8,128)(2,1)S(1)}, bf16[512,2048]{1,0:T(8,128)(2,1)}, u32[]{:S(2)}) copy-start(bf16[512,2048]{1,0:T(8,128)(2,1)} %param.21) | copy-start | bytes 6291460
  7.2 7.9 copy-start.40
  7.2 42.6 %all-gather.4.cloned.1.call-start = ((), (), s32[]{:S(2)}) async-start(), calls=%async_computation.8 | async-start | bytes 2359296 | tf_op jit(solution)/shard_map/all_gather | solution.py:110
  10.1 9.4 copy-start.50
  10.9 4.2 copy-start.26
  12.5 6.9 copy-start.48
  12.5 3.6 copy-start.57
  17.0 6.0 copy-start.37
  17.9 273.7 %all-gather.6.cloned.1.call-start = ((), (), s32[]{:S(2)}) async-start(), calls=%async_computation.18 | async-start | bytes 20971520 | tf_op jit(solution)/shard_map/all_gather | solution.py:152
  19.3 409.9 %copy-start.53 = (pred[512]{0:T(512)(128)(4,1)}, pred[512]{0:T(512)(128)(4,1)S(1)}, u32[]{:S(2)}) copy-start(pred[512]{0:T(512)(128)(4,1)S(1)} %fusion.150) | copy-start | bytes 1540
  53.4 3.3 copy-start.7
  61.7 64.6 %copy-start.4 = (f32[512,4096]{1,0:T(8,128)}, f32[512,4096]{1,0:T(8,128)S(1)}, u32[]{:S(2)}) copy-start(f32[512,4096]{1,0:T(8,128)S(1)} %get-tuple-element.136) | copy-start | bytes 25165828
  89.0 25.9 %copy-start.5 = (f32[512,4096]{1,0:T(8,128)}, f32[512,4096]{1,0:T(8,128)S(1)}, u32[]{:S(2)}) copy-start(f32[512,4096]{1,0:T(8,128)S(1)} %get-tuple-element.128) | copy-start | bytes 25165828
  94.8 18.3 %copy-start.6 = (f32[512,4096]{1,0:T(8,128)}, f32[512,4096]{1,0:T(8,128)S(1)}, u32[]{:S(2)}) copy-start(f32[512,4096]{1,0:T(8,128)S(1)} %get-tuple-element.126) | copy-start | bytes 25165828
  103.2 4.8 copy-start.24
  114.9 7.2 slice-start.16
  116.7 5.4 slice-start.17
  116.7 7.2 slice-start.10
  124.4 3.7 slice-start.6
  131.2 3.4 copy-start.56
  134.5 286.2 %all-reduce.7.cloned.1.call-start = ((), (), s32[]{:S(2)}) async-start(), calls=%async_computation.9 | async-start | bytes 4194304 | tf_op jit(solution)/shard_map/psum | solution.py:175
  305.2 10.1 copy-start.2
  305.2 10.1 slice-start.22
  305.7 9.7 copy-start.35
  305.7 9.7 slice-start.23
  315.4 6.3 copy-start.36
  333.6 7.8 copy-start.59
  350.8 282.9 %reduce-scatter.9.cloned.1.call-start = ((), (), s32[]{:S(2)}) async-start(), calls=%async_computation.10 | async-start | bytes 2359296 | tf_op jit(solution)/shard_map/reduce_scatter | solution.py:225
  420.7 4.9 copy-start.3
  420.7 10.7 slice-start.14
  425.6 5.8 slice-start.15
  429.2 4.6 slice-start.18
  431.4 5.4 slice-start.4
  434.4 4.9 slice-start.2
  434.4 8.7 slice-start.20
  436.8 3.6 slice-start.3
  436.8 6.2 slice-start.21
  440.4 6.0 slice-start.12
  440.4 8.4 slice-start
  443.1 3.3 slice-start.13
  443.1 5.8 slice-start.1
  446.4 4.9 slice-start.8
  451.3 3.3 copy-start.25
  531.2 23.4 %copy-start.34 = (bf16[512,8,2,32]{0,3,2,1:T(8,128)(2,1)S(1)}, bf16[512,8,2,32]{0,3,2,1:T(8,128)(2,1)}, u32[]{:S(2)}) copy-start(bf16[512,8,2,32]{0,3,2,1:T(8,128)(2,1)} %pad_maximum_fusion.1) | copy-start | bytes 1572868
  583.4 3.5 copy-start.13
  583.4 3.7 copy-start.33
  597.8 90.0 %reduce-scatter.17.cloned.1.call-start = ((), (), s32[]{:S(2)}) async-start(), calls=%async_computation.14 | async-start | bytes 2359296 | tf_op jit(solution)/shard_map/reduce_scatter | solution.py:257
  602.7 104.4 %reduce-scatter.11.cloned.1.call-start = ((), (), s32[]{:S(2)}) async-start(), calls=%async_computation.11 | async-start | bytes 2359296 | tf_op jit(solution)/shard_map/reduce_scatter | solution.py:248
  602.7 7.7 copy-start.22
  606.6 5.2 copy-start.18
  619.3 15.4 %copy-start.28 = (bf16[512,2048]{1,0:T(8,128)(2,1)S(1)}, bf16[512,2048]{1,0:T(8,128)(2,1)}, u32[]{:S(2)}) copy-start(bf16[512,2048]{1,0:T(8,128)(2,1)} %param.16) | copy-start | bytes 6291460
  622.2 116.8 %reduce-scatter.13.cloned.1.call-start = ((), (), s32[]{:S(2)}) async-start(), calls=%async_computation.12 | async-start | bytes 589824 | tf_op jit(solution)/shard_map/reduce_scatter | solution.py:251
  636.6 133.9 %reduce-scatter.15.cloned.1.call-start = ((), (), s32[]{:S(2)}) async-start(), calls=%async_computation.13 | async-start | bytes 589824 | tf_op jit(solution)/shard_map/reduce_scatter | solution.py:254
  637.0 10.0 copy-start.47
  648.9 228.5 %all-reduce.9.cloned.1.call-start = ((), (), s32[]{:S(2)}) async-start(), calls=%async_computation.19 | async-start | bytes 8388608 | tf_op jit(solution)/shard_map/psum | solution.py:173
  655.1 314.5 %reduce-scatter.21.cloned.1.call-start = ((), (), s32[]{:S(2)}) async-start(), calls=%async_computation.16 | async-start | bytes 9437184 | tf_op jit(solution)/shard_map/reduce_scatter | solution.py:266
  665.3 394.6 %reduce-scatter.19.cloned.1.call-start = ((), (), s32[]{:S(2)}) async-start(), calls=%async_computation.15 | async-start | bytes 9437184 | tf_op jit(solution)/shard_map/reduce_scatter | solution.py:263
  675.6 474.4 %reduce-scatter.23.cloned.1.call-start = ((), (), s32[]{:S(2)}) async-start(), calls=%async_computation.17 | async-start | bytes 9437184 | tf_op jit(solution)/shard_map/reduce_scatter | solution.py:269
  685.9 194.6 %copy-start.52 = (bf16[2048]{0:T(1024)(128)(2,1)S(1)}, bf16[2048]{0:T(1024)(128)(2,1)}, u32[]{:S(2)}) copy-start(bf16[2048]{0:T(1024)(128)(2,1)} %get-tuple-element.65) | copy-start | bytes 12292
  707.1 197.2 %copy-start.55 = (f32[512]{0:T(512)S(1)}, f32[512]{0:T(512)}, u32[]{:S(2)}) copy-start(f32[512]{0:T(512)} %get-tuple-element.119) | copy-start | bytes 6148
  899.2 5.1 copy-start.29
  899.2 5.1 copy-start.31
  899.2 6.2 copy-start.32
  905.4 247.2 %copy-start.1 = (bf16[512,2048]{1,0:T(8,128)(2,1)S(1)}, bf16[512,2048]{1,0:T(8,128)(2,1)}, u32[]{:S(2)}) copy-start(bf16[512,2048]{1,0:T(8,128)(2,1)} %param.21) | copy-start | bytes 6291460
  (32 other events, 72.7 us)
Sparse Core Ops, SparseCore 0:
  18.0 31.7 all-gather.3
  134.6 156.8 all-gather.5
  351.0 69.6 all-reduce.6
  597.9 35.7 reduce-scatter.8
  635.9 34.4 reduce-scatter.16
  672.7 34.3 reduce-scatter.10
  709.4 29.5 reduce-scatter.12
  741.3 29.1 reduce-scatter.14
  774.9 102.4 all-reduce.8
  879.5 90.0 reduce-scatter.20
  971.9 87.8 reduce-scatter.18
  1062.0 87.9 reduce-scatter.22
